TPU v7x, 32 devices: a whole 2x2x4 slice. The times are simulated.
32 devices in a mesh: rows: 4 (over y, core), dp: 8 (over z, x).
Axes of the slice: x: 2, y: 2, z: 4, core: 2. Of those that a mesh axis runs over, the one named last changes fastest.
Arguments:
- emb_weight: float32 [8, 6144, 128], P('dp', 'rows'), may hold values from -160 to 160
- emb_grad: bfloat16 [8, 6144, 128], P('dp', 'rows'), may hold values from -6 to 6
- emb_moment: float32 [8, 6144, 128], P('dp', 'rows'), may hold values from -160 to 160
- emb_second: float32 [8, 6144, 128], P('dp', 'rows'), may hold values from 0.1 to 4
- hot_rows: int32 [8, 4, 256], P('dp', 'rows'), may hold values from 0 to 1535
- block_counts: int32 [8, 4], P('dp', 'rows'), may hold values from 1 to 2, as said below
- dense_weight: float32 [512, 256], replicated, may hold values from -8 to 8
- dense_grad: float32 [32, 512, 256], P(('rows', 'dp')), may hold values from -6 to 6
- dense_moment: float32 [512, 256], replicated, may hold values from -900 to 900
- dense_second: float32 [512, 256], replicated, may hold values from 3.2 to 128
Outputs:
- new_weight: float32 [8, 6144, 128], P('dp', 'rows')
- new_moment: float32 [8, 6144, 128], P('dp', 'rows')
- new_second: float32 [8, 6144, 128], P('dp', 'rows')
- hot_cache: bfloat16 [8, 4, 256, 128], P(None, 'rows')
- fresh_dense: float32 [512, 256], replicated
- fresh_moment: float32 [512, 256], replicated
- fresh_second: float32 [512, 256], replicated
Inputs may be any that keep to these rules, and one draw needn't show every extreme that they name: `block_counts`: some table shard has 2 live blocks in every draw. `hot_rows`: entries in dead blocks are ignored.
All inputs are finite; a program needn't handle non-finite values.
Results may differ from a plain program's by a relative error of at most 0.001.
Values may be sent and summed in bfloat16 or wider, within the bound.
A program may use at most 64 MiB of HBM per device.

v0:
```python
import jax
import jax.numpy as jnp
from jax import lax
from jax.sharding import PartitionSpec as P

BLOCK = 128
beta_one = 0.9
beta_two = 0.999
first_fix = 1.0 / (1.0 - 0.9**10)
second_fix = 1.0 / (1.0 - 0.999**10)
epsilon = 1e-06
norm_floor = 1e-06
decay_rate = 0.1
learn_rate = 0.05


def moments(gradient, moment, second):
    new_moment = beta_one * moment + (1.0 - beta_one) * gradient
    new_second = beta_two * second + (1.0 - beta_two) * gradient * gradient
    direction = first_fix * new_moment / (jnp.sqrt(second_fix * new_second) + epsilon)
    return (new_moment, new_second, direction)


def trust_step(weight_sq, update_sq):
    return learn_rate * jnp.sqrt(weight_sq + norm_floor) / jnp.sqrt(update_sq + norm_floor)


def pick_rows(source, row_ids, live_mask):
    picked = jnp.take_along_axis(source, row_ids[:, :, None], axis=1)
    return jnp.where(live_mask, picked, jnp.zeros_like(picked))


def shards(
    emb_weight,
    emb_grad,
    emb_moment,
    emb_second,
    hot_rows,
    block_counts,
    dense_weight,
    dense_grad,
    dense_moment,
    dense_second,
):
    new_moment, new_second, direction = moments(
        emb_grad.astype(jnp.float32), emb_moment, emb_second
    )
    update = direction + decay_rate * emb_weight
    weight_sq = jnp.sum(emb_weight * emb_weight, axis=(1, 2))
    update_sq = jnp.sum(update * update, axis=(1, 2))
    row_ids = hot_rows[:, 0, :]
    live_mask = (
        jnp.arange(row_ids.shape[1], dtype=jnp.int32)[None, :] < BLOCK * block_counts[:, 0][:, None]
    )[:, :, None]
    weight_sq, update_sq = lax.psum((weight_sq, update_sq), "rows")
    summed_grad = lax.psum(dense_grad[0], ("rows", "dp"))
    step_size = trust_step(weight_sq, update_sq)
    new_weight = emb_weight - step_size[:, None, None] * update
    fresh_rows = pick_rows(new_weight, row_ids, live_mask).astype(jnp.bfloat16)
    hot_cache = lax.all_gather(fresh_rows[:, None], "dp", axis=0, tiled=True)
    fresh_moment, fresh_second, heading = moments(summed_grad, dense_moment, dense_second)
    dense_scale = trust_step(jnp.sum(dense_weight * dense_weight), jnp.sum(heading * heading))
    fresh_dense = dense_weight - dense_scale * heading
    return (new_weight, new_moment, new_second, hot_cache, fresh_dense, fresh_moment, fresh_second)


def solution(mesh):
    in_specs = (
        P("dp", "rows", None),
        P("dp", "rows", None),
        P("dp", "rows", None),
        P("dp", "rows", None),
        P("dp", "rows", None),
        P("dp", "rows"),
        P(),
        P(("rows", "dp"), None, None),
        P(),
        P(),
    )
    out_specs = (
        P("dp", "rows", None),
        P("dp", "rows", None),
        P("dp", "rows", None),
        P(None, "rows", None, None),
        P(),
        P(),
        P(),
    )
    return jax.shard_map(shards, mesh=mesh, in_specs=in_specs, out_specs=out_specs, check_vma=False)
```

profile of v0, /device:TPU:0, one launch (start us, length us, event | category | flops | bytes accessed | tf_op | source)
XLA Modules:
  0.0 157.2 jit_solution(17195900723018866183)
XLA Ops:
  7.2 0.0 copy-start.7
  7.2 0.0 all-reduce.3.cloned.1.call-start
  7.2 0.7 all-reduce.3.cloned.1.call-update
  7.9 0.3 copy-done.7
  8.2 0.0 copy-start
  8.2 3.0 %multiply_reduce_fusion = (f32[]{:T(128)}, f32[]{:T(128)}, f32[1,1536,128]{2,1,0:T(8,128)S(1)}, f32[1,1536,128]{2,1,0:T(8,128)S(1)}) fusion(f32[1,1536,128]{2,1,0:T(8,128)} %param.10, bf16[1,1536,128]{2,1,0:T(8,128)(2,1)S(1)} %copy-done.7, f32[1,1536,128]{2,1,0:T(8,128)} %param.12, f32[1,1536,128]{2,1,0:T(8,128)} %param.13), kind=kLoop, calls=%fused_computation.7 | loop fusion | flops 3538942 | bytes 4325384 | tf_op jit(solution)/shard_map/reduce_sum | solution.py:50
  11.1 0.0 copy-start.1
  11.1 0.0 copy-start.2
  11.1 9.0 %all-reduce = (f32[1]{0:T(128)}, f32[1]{0:T(128)}) all-reduce(f32[1]{0:T(128)} %bitcast, f32[1]{0:T(128)} %bitcast.1), channel_id=1, replica_groups=mesh['rows'=4,'dp'=8] {'rows'}, use_global_device_ids=true, to_apply=%region_1.0 | all-reduce | flops 2 | bytes 16 | tf_op jit(solution)/shard_map/psum | solution.py:55
  21.5 0.0 copy-start.8
  21.5 0.6 copy-done.8
  22.8 0.0 copy-done
  22.8 0.4 multiply_subtract_fusion
  23.3 0.0 copy-done.1
  23.3 0.0 copy-done.2
  23.3 0.0 copy-start.3
  23.3 0.0 copy-start.4
  23.3 0.7 gather_fusion
  24.1 0.1 fusion.4
  24.2 32.1 %all_gather.3 = bf16[8,1,256,128]{3,2,1,0:T(8,128)(2,1)S(1)} all-gather(bf16[1,1,256,128]{3,2,1,0:T(8,128)(2,1)S(1)} %fusion.4), channel_id=1, replica_groups=mesh['rows'=4,'dp'=8] {'dp'}, dimensions={0}, use_global_device_ids=true | all-gather | bytes 589824 | tf_op jit(solution)/shard_map/all_gather | solution.py:60
  56.3 0.0 copy-done.4
  56.3 0.7 multiply_reduce_fusion.3
  57.0 0.0 copy-done.3
  57.7 87.8 %all-reduce.3.cloned.1.call-done = f32[512,256]{1,0:T(8,128)} async-done(((f32[512,256]{1,0:T(8,128)}), f32[512,256]{1,0:T(8,128)}) %all-reduce.3.cloned.1.call-update) | async-done | bytes 524304 | tf_op jit(solution)/shard_map/psum | solution.py:56
  145.5 2.3 %multiply_reduce_fusion.2 = (f32[]{:T(128)}, f32[512,256]{1,0:T(8,128)S(1)}, f32[512,256]{1,0:T(8,128)S(1)}) fusion(f32[512,256]{1,0:T(8,128)} %all-reduce.3.cloned.1.call-done, f32[512,256]{1,0:T(8,128)} %param.18, f32[512,256]{1,0:T(8,128)} %param.19), kind=kLoop, calls=%fused_computation.12 | loop fusion | flops 1703935 | bytes 2621444 | tf_op jit(solution)/shard_map/reduce_sum | solution.py:62
  147.8 0.0 copy-start.5
  147.8 0.0 copy-start.6
  148.5 1.0 multiply_subtract_fusion.1
  149.6 0.0 copy-done.5
  149.6 0.0 copy-done.6
  149.6 0.8 copy.21
  (3 shorter events, 0.0 us)
Async XLA Ops:
  7.2 1.0 copy-start.7
  7.2 138.3 %all-reduce.3.cloned.1.call-start = ((), (), s32[]{:S(2)}) async-start(), calls=%async_computation | async-start | bytes 1048576 | tf_op jit(solution)/shard_map/psum | solution.py:56
  8.2 14.7 %copy-start = (f32[1,1536,128]{2,1,0:T(8,128)S(1)}, f32[1,1536,128]{2,1,0:T(8,128)}, u32[]{:S(2)}) copy-start(f32[1,1536,128]{2,1,0:T(8,128)} %param.10) | copy-start | bytes 2359300
  11.1 12.2 %copy-start.1 = (f32[1,1536,128]{2,1,0:T(8,128)}, f32[1,1536,128]{2,1,0:T(8,128)S(1)}, u32[]{:S(2)}) copy-start(f32[1,1536,128]{2,1,0:T(8,128)S(1)} %get-tuple-element.26) | copy-start | bytes 2359300
  11.1 12.2 %copy-start.2 = (f32[1,1536,128]{2,1,0:T(8,128)}, f32[1,1536,128]{2,1,0:T(8,128)S(1)}, u32[]{:S(2)}) copy-start(f32[1,1536,128]{2,1,0:T(8,128)S(1)} %get-tuple-element.27) | copy-start | bytes 2359300
  21.5 0.7 copy-start.8
  23.3 33.7 %copy-start.3 = (f32[1,1536,128]{2,1,0:T(8,128)}, f32[1,1536,128]{2,1,0:T(8,128)S(1)}, u32[]{:S(2)}) copy-start(f32[1,1536,128]{2,1,0:T(8,128)S(1)} %multiply_subtract_fusion) | copy-start | bytes 2359300
  23.3 33.0 %copy-start.4 = (f32[512,256]{1,0:T(8,128)S(1)}, f32[512,256]{1,0:T(8,128)}, u32[]{:S(2)}) copy-start(f32[512,256]{1,0:T(8,128)} %param.16) | copy-start | bytes 1572868
  147.8 1.7 %copy-start.5 = (f32[512,256]{1,0:T(8,128)}, f32[512,256]{1,0:T(8,128)S(1)}, u32[]{:S(2)}) copy-start(f32[512,256]{1,0:T(8,128)S(1)} %get-tuple-element.30) | copy-start | bytes 1572868
  147.8 1.7 %copy-start.6 = (f32[512,256]{1,0:T(8,128)}, f32[512,256]{1,0:T(8,128)S(1)}, u32[]{:S(2)}) copy-start(f32[512,256]{1,0:T(8,128)S(1)} %get-tuple-element.31) | copy-start | bytes 1572868
Sparse Core Ops, SparseCore 0:
  13.3 132.1 all-reduce.2
where the time goes:
time: 158 us; the launch traced here: 157 us
  waiting for transfers between devices  88.4 us (56%)
  blocking collectives  41.1 us (26%)
  between operations  17.5 us (11%)
  other arithmetic  7.64 us (5%)
  local copies, waits for them, and re-layouts  2.46 us (2%)
    psum x1, waiting for transfers between devices, shards(): summed_grad = lax.psum(dense_grad[0], ('rows', 'dp'))  87.8 us
    all_gather x1, blocking collectives, shards(): hot_cache = lax.all_gather(fresh_rows[:, None], 'dp', axis=0, tiled=True)  32.1 us
    psum x1, blocking collectives, shards(): weight_sq, update_sq = lax.psum((weight_sq, update_sq), 'rows')  9.01 us
  transfers between devices with their start and end apart: 1, of which 1 were waited for; matrix products, arithmetic and copies ran while one was open for 3% of the time, Pallas kernels for 0%

commit v1 on v0

--- a/solution.py
+++ b/solution.py
@@ -53,7 +53,8 @@
         jnp.arange(row_ids.shape[1], dtype=jnp.int32)[None, :] < BLOCK * block_counts[:, 0][:, None]
     )[:, :, None]
     weight_sq, update_sq = lax.psum((weight_sq, update_sq), "rows")
-    summed_grad = lax.psum(dense_grad[0], ("rows", "dp"))
+    own_rows = dense_grad[0]
+    summed_grad = lax.psum(lax.psum(own_rows, "dp"), "rows")
     step_size = trust_step(weight_sq, update_sq)
     new_weight = emb_weight - step_size[:, None, None] * update
     fresh_rows = pick_rows(new_weight, row_ids, live_mask).astype(jnp.bfloat16)

time: 158 us -> 134 us (0.85)
  waiting for transfers between devices: 88.4 us -> 65.4 us
    psum x1 -> x2, waiting for transfers between devices: 87.8 us -> 64.7 us  [shards(): summed_grad = lax.psum(lax.psum(own_rows, 'dp'), 'rows')]
  transfers between devices with their start and end apart: 1 -> 2, of which waited for: 1 -> 2; matrix products, arithmetic and copies ran while one was open for 3% -> 4% of each run, Pallas kernels for 0% -> 0%
where the time goes in v1:
time: 134 us; the launch traced here: 133 us
  waiting for transfers between devices  65.4 us (49%)
  blocking collectives  40.6 us (30%)
  between operations  17.6 us (13%)
  other arithmetic  7.25 us (5%)
  local copies, waits for them, and re-layouts  2.41 us (2%)
    psum x2, waiting for transfers between devices, shards(): summed_grad = lax.psum(lax.psum(own_rows, 'dp'), 'rows')  64.7 us
    all_gather x1, blocking collectives, shards(): hot_cache = lax.all_gather(fresh_rows[:, None], 'dp', axis=0, tiled=True)  31.6 us
    psum x1, blocking collectives, shards(): weight_sq, update_sq = lax.psum((weight_sq, update_sq), 'rows')  9.01 us
    reduce_sum x1, other arithmetic, shards(): update_sq = jnp.sum(update * update, axis=(1, 2))  2.88 us
  transfers between devices with their start and end apart: 2, of which 2 were waited for; matrix products, arithmetic and copies ran while one was open for 4% of the time, Pallas kernels for 0%

profile of v1, /device:TPU:0, one launch (start us, length us, event | category | flops | bytes accessed | tf_op | source)
XLA Modules:
  0.0 133.3 jit_solution(7645916884338954462)
XLA Ops:
  7.2 0.0 copy-start.9
  7.2 0.0 all-reduce.4.cloned.1.call-start
  7.2 0.7 all-reduce.4.cloned.1.call-update
  7.9 0.0 copy-start
  7.9 0.0 all-reduce.6.cloned.1.call-start
  8.0 0.2 copy-done.9
  8.2 2.9 %multiply_reduce_fusion = (f32[]{:T(128)}, f32[]{:T(128)}, f32[1,1536,128]{2,1,0:T(8,128)S(1)}, f32[1,1536,128]{2,1,0:T(8,128)S(1)}) fusion(f32[1,1536,128]{2,1,0:T(8,128)} %param.10, bf16[1,1536,128]{2,1,0:T(8,128)(2,1)S(1)} %copy-done.9, f32[1,1536,128]{2,1,0:T(8,128)} %param.12, f32[1,1536,128]{2,1,0:T(8,128)} %param.13), kind=kLoop, calls=%fused_computation.7 | loop fusion | flops 3538942 | bytes 4325384 | tf_op jit(solution)/shard_map/reduce_sum | solution.py:50
  11.0 0.0 copy-start.1
  11.1 0.0 copy-start.2
  11.1 9.0 %all-reduce = (f32[1]{0:T(128)}, f32[1]{0:T(128)}) all-reduce(f32[1]{0:T(128)} %bitcast, f32[1]{0:T(128)} %bitcast.1), channel_id=1, replica_groups=mesh['rows'=4,'dp'=8] {'rows'}, use_global_device_ids=true, to_apply=%region_1.0 | all-reduce | flops 2 | bytes 16 | tf_op jit(solution)/shard_map/psum | solution.py:55
  21.4 0.0 copy-start.10
  21.5 0.6 copy-done.10
  22.8 0.0 copy-done
  22.8 0.4 multiply_subtract_fusion
  23.2 0.0 copy-done.1
  23.2 0.0 copy-done.2
  23.2 0.0 copy-start.3
  23.2 0.7 gather_fusion
  24.0 0.1 fusion.4
  24.1 62.8 %all-reduce.4.cloned.1.call-done = f32[512,256]{1,0:T(8,128)} async-done(((f32[512,256]{1,0:T(8,128)}), f32[512,256]{1,0:T(8,128)}) %all-reduce.4.cloned.1.call-update) | async-done | bytes 524304 | tf_op jit(solution)/shard_map/psum | solution.py:57
  86.9 0.0 copy-start.4
  86.9 0.0 all-reduce.6.cloned.1.call-update
  87.0 0.0 copy-start.7
  87.0 0.0 copy-start.8
  87.0 31.6 %all_gather.3 = bf16[8,1,256,128]{3,2,1,0:T(8,128)(2,1)S(1)} all-gather(bf16[1,1,256,128]{3,2,1,0:T(8,128)(2,1)S(1)} %fusion.4), channel_id=1, replica_groups=mesh['rows'=4,'dp'=8] {'dp'}, dimensions={0}, use_global_device_ids=true | all-gather | bytes 589824 | tf_op jit(solution)/shard_map/all_gather | solution.py:61
  118.6 0.0 copy-done.3
  118.6 0.0 copy-done.4
  118.6 0.7 multiply_reduce_fusion.3
  120.0 1.9 %all-reduce.6.cloned.1.call-done = f32[512,256]{1,0:T(8,128)} async-done(((f32[512,256]{1,0:T(8,128)}), f32[512,256]{1,0:T(8,128)}) %all-reduce.6.cloned.1.call-update) | async-done | bytes 524304 | tf_op jit(solution)/shard_map/psum | solution.py:57
  121.9 0.0 copy-done.7
  121.9 0.0 copy-done.8
  121.9 2.0 %multiply_reduce_fusion.2 = (f32[]{:T(128)}, f32[512,256]{1,0:T(8,128)S(1)}, f32[512,256]{1,0:T(8,128)S(1)}) fusion(f32[512,256]{1,0:T(8,128)} %all-reduce.6.cloned.1.call-done, f32[512,256]{1,0:T(8,128)S(1)} %copy-done.7, f32[512,256]{1,0:T(8,128)S(1)} %copy-done.8), kind=kLoop, calls=%fused_computation.12 | loop fusion | flops 1703935 | bytes 2621444 | tf_op jit(solution)/shard_map/reduce_sum | solution.py:63
  123.9 0.0 copy-start.5
  123.9 0.0 copy-start.6
  124.6 1.0 multiply_subtract_fusion.1
  125.7 0.0 copy-done.5
  125.7 0.0 copy-done.6
  125.7 0.8 copy.22
  (3 shorter events, 0.0 us)
Async XLA Ops:
  7.2 1.0 copy-start.9
  7.2 79.8 %all-reduce.4.cloned.1.call-start = ((), (), s32[]{:S(2)}) async-start(), calls=%async_computation | async-start | bytes 1048576 | tf_op jit(solution)/shard_map/psum | solution.py:57
  7.9 14.8 %copy-start = (f32[1,1536,128]{2,1,0:T(8,128)S(1)}, f32[1,1536,128]{2,1,0:T(8,128)}, u32[]{:S(2)}) copy-start(f32[1,1536,128]{2,1,0:T(8,128)} %param.10) | copy-start | bytes 2359300
  7.9 114.0 %all-reduce.6.cloned.1.call-start = ((), (), s32[]{:S(2)}) async-start(), calls=%async_computation.1 | async-start | bytes 1048576 | tf_op jit(solution)/shard_map/psum | solution.py:57
  11.0 12.1 %copy-start.1 = (f32[1,1536,128]{2,1,0:T(8,128)}, f32[1,1536,128]{2,1,0:T(8,128)S(1)}, u32[]{:S(2)}) copy-start(f32[1,1536,128]{2,1,0:T(8,128)S(1)} %get-tuple-element.26) | copy-start | bytes 2359300
  11.1 12.1 %copy-start.2 = (f32[1,1536,128]{2,1,0:T(8,128)}, f32[1,1536,128]{2,1,0:T(8,128)S(1)}, u32[]{:S(2)}) copy-start(f32[1,1536,128]{2,1,0:T(8,128)S(1)} %get-tuple-element.27) | copy-start | bytes 2359300
  21.4 0.7 copy-start.10
  23.2 95.4 %copy-start.3 = (f32[1,1536,128]{2,1,0:T(8,128)}, f32[1,1536,128]{2,1,0:T(8,128)S(1)}, u32[]{:S(2)}) copy-start(f32[1,1536,128]{2,1,0:T(8,128)S(1)} %multiply_subtract_fusion) | copy-start | bytes 2359300
  86.9 31.6 %copy-start.4 = (f32[512,256]{1,0:T(8,128)S(1)}, f32[512,256]{1,0:T(8,128)}, u32[]{:S(2)}) copy-start(f32[512,256]{1,0:T(8,128)} %param.16) | copy-start | bytes 1572868
  87.0 34.9 %copy-start.7 = (f32[512,256]{1,0:T(8,128)S(1)}, f32[512,256]{1,0:T(8,128)}, u32[]{:S(2)}) copy-start(f32[512,256]{1,0:T(8,128)} %param.18) | copy-start | bytes 1572868
  87.0 34.9 %copy-start.8 = (f32[512,256]{1,0:T(8,128)S(1)}, f32[512,256]{1,0:T(8,128)}, u32[]{:S(2)}) copy-start(f32[512,256]{1,0:T(8,128)} %param.19) | copy-start | bytes 1572868
  123.9 1.7 %copy-start.5 = (f32[512,256]{1,0:T(8,128)}, f32[512,256]{1,0:T(8,128)S(1)}, u32[]{:S(2)}) copy-start(f32[512,256]{1,0:T(8,128)S(1)} %get-tuple-element.30) | copy-start | bytes 1572868
  123.9 1.7 %copy-start.6 = (f32[512,256]{1,0:T(8,128)}, f32[512,256]{1,0:T(8,128)S(1)}, u32[]{:S(2)}) copy-start(f32[512,256]{1,0:T(8,128)S(1)} %get-tuple-element.31) | copy-start | bytes 1572868
Sparse Core Ops, SparseCore 0:
  11.4 75.4 all-reduce.3
  89.3 32.5 all-reduce.5
